TPU v7x, 256 devices: a whole 4x4x8 slice. The times are simulated.
256 devices in a mesh: tile: 32 (over x, z), slide: 8 (over y, core).
Axes of the slice: x: 4, y: 4, z: 8, core: 2. Of those that a mesh axis runs over, the one named last changes fastest.
Arguments:
- tiles: bfloat16 [8, 96, 7, 7, 2048], P('slide', 'tile'), may hold values from -6 to 6
- tile_counts: int32 [8, 32], P('slide', 'tile'), may hold values from 1 to 3, as said below
- tile_weights: float32 [8, 96], P('slide', 'tile'), may hold values from 0.1 to 2
- slide_of: int32 [8, 96, 1], P('slide', 'tile'), may hold values from 0 to 31, as said below
- owner_map: int32 [8, 32], P('slide'), may hold values from 0 to 31, each once within a row
- cotangent: bfloat16 [8, 32, 2048], P('slide', 'tile'), may hold values from -6 to 6
- conv_weight: bfloat16 [9, 64, 2048], replicated, may hold values from -0.25 to 0.25
Outputs:
- pooled: float32 [8, 32, 2048], P('slide', 'tile')
- input_grads: float32 [8, 96, 7, 7, 2048], P('slide', 'tile')
- weight_grads: float32 [9, 64, 2048], P(None, None, 'tile')
Inputs may be any that keep to these rules, and one draw needn't show every extreme that they name: On every device the live tiles are the first tile_counts slots; in each slide group one device has all 3 slots live. `slide_of`: in each slide group, max(1, 8) slides name exactly one slot each, the first slot of some device; the other slots name the remaining slides evenly at random.
All inputs are finite; a program needn't handle non-finite values.
Results may differ from a plain program's by a relative error of at most 0.0065.
Values may be sent and summed in bfloat16 or wider, within the bound.
A program may use at most 128 MiB of HBM per device.

v0:
```python
import jax
import jax.numpy as jnp
from jax import lax
from jax.sharding import PartitionSpec as P

loss_scale = 512.0


def conv_forward(features, weight):
    count_rows, spatial = (features.shape[0], features.shape[1])
    group_width, channels = (weight.shape[1], weight.shape[2])
    groups = channels // group_width
    padded = jnp.pad(features, ((0, 0), (1, 1), (1, 1), (0, 0)))
    summed = jnp.zeros((count_rows, spatial, spatial, groups, group_width), jnp.float32)
    for offset in range(9):
        row_off, col_off = divmod(offset, 3)
        window = padded[:, row_off : row_off + spatial, col_off : col_off + spatial, :].reshape(
            count_rows, spatial, spatial, groups, group_width
        )
        tap = weight[offset].reshape(group_width, groups, group_width)
        summed = summed + jnp.einsum(
            "nhwgi,igo->nhwgo", window, tap, preferred_element_type=jnp.float32
        )
    return summed.reshape(count_rows, spatial, spatial, channels)


def conv_backward(features, weight, pre_grad):
    count_rows, spatial = (features.shape[0], features.shape[1])
    group_width, channels = (weight.shape[1], weight.shape[2])
    groups = channels // group_width
    padded = jnp.pad(features, ((0, 0), (1, 1), (1, 1), (0, 0)))
    grads_split = pre_grad.reshape(count_rows, spatial, spatial, groups, group_width)
    grads_padded = jnp.pad(grads_split, ((0, 0), (1, 1), (1, 1), (0, 0), (0, 0)))
    summed = jnp.zeros((count_rows, spatial, spatial, groups, group_width), jnp.float32)
    pieces = []
    for offset in range(9):
        row_off, col_off = divmod(offset, 3)
        window = padded[:, row_off : row_off + spatial, col_off : col_off + spatial, :].reshape(
            count_rows, spatial, spatial, groups, group_width
        )
        tap = weight[offset].reshape(group_width, groups, group_width)
        pieces.append(
            jnp.einsum(
                "nhwgi,nhwgo->igo", window, grads_split, preferred_element_type=jnp.float32
            ).reshape(group_width, channels)
        )
        shifted = grads_padded[
            :, 2 - row_off : 2 - row_off + spatial, 2 - col_off : 2 - col_off + spatial
        ]
        summed = summed + jnp.einsum(
            "nhwgo,igo->nhwgi", shifted, tap, preferred_element_type=jnp.float32
        )
    input_grads = summed.reshape(count_rows, spatial, spatial, channels)
    return (input_grads, jnp.stack(pieces, axis=0))


def shards(tiles, tile_counts, tile_weights, slide_of, owner_map, cotangent, conv_weight):
    features = tiles[0]
    slots = features.shape[0]
    spatial = features.shape[1]
    tile_total = lax.axis_size("tile")
    my_index = lax.axis_index("tile")
    alive = (jnp.arange(slots, dtype=jnp.int32) < tile_counts[0, 0]).astype(jnp.float32)
    tile_coef = alive * tile_weights[0]
    owner_ids = jnp.arange(tile_total, dtype=jnp.int32)
    slide_hits = slide_of[0, :, 0][:, None] == owner_ids[None, :]
    target = jnp.sum(jnp.where(slide_hits, owner_map[0][None, :], 0), axis=1)
    routing = (target[None, :] == owner_ids[:, None]).astype(jnp.float32) * tile_coef[None, :]
    pre = conv_forward(features, conv_weight)
    embedding = jnp.mean(jax.nn.silu(pre), axis=(1, 2)).astype(jnp.bfloat16)
    shares = lax.all_gather(routing, "tile", axis=1, tiled=True)
    own_row = lax.dynamic_slice_in_dim(shares, my_index, 1, 0)
    numerator = jnp.dot(
        own_row,
        lax.all_gather(embedding, "tile", axis=0, tiled=True).astype(jnp.float32),
        precision=lax.Precision.HIGHEST,
    )
    weight_total = jnp.sum(own_row, axis=1)
    denominator = jnp.maximum(weight_total, 1.0)
    pooled = numerator / denominator[:, None]
    scaled = (loss_scale * cotangent[0].astype(jnp.float32) / denominator[:, None]).astype(
        jnp.bfloat16
    )
    every_scaled = lax.all_gather(scaled, "tile", axis=0, tiled=True)
    tile_grads = jnp.dot(
        routing.T, every_scaled.astype(jnp.float32), precision=lax.Precision.HIGHEST
    )
    sigma = jax.nn.sigmoid(pre)
    slope = sigma * (1.0 + pre * (1.0 - sigma))
    pre_grad = (tile_grads[:, None, None, :] / (spatial * spatial) * slope).astype(jnp.bfloat16)
    input_grads, weight_terms = conv_backward(features, conv_weight, pre_grad)
    shard_sum = lax.psum_scatter(weight_terms, "tile", scatter_dimension=2, tiled=True)
    reduced = lax.psum(shard_sum, "slide")
    return (pooled[None], input_grads[None], reduced / loss_scale)


def solution(mesh):
    return jax.shard_map(
        shards,
        mesh=mesh,
        in_specs=(
            P("slide", "tile", None, None, None),
            P("slide", "tile"),
            P("slide", "tile"),
            P("slide", "tile", None),
            P("slide", None),
            P("slide", "tile", None),
            P(),
        ),
        out_specs=(
            P("slide", "tile", None),
            P("slide", "tile", None, None, None),
            P(None, None, "tile"),
        ),
        check_vma=False,
    )
```

profile of v0, /device:TPU:2, one launch (start us, length us, event | category | flops | bytes accessed | tf_op | source)
XLA Modules:
  0.0 547.1 jit_solution(8483302812085023196)
XLA Ops:
  9.5 51.4 %all-gather.1 = f32[32,3,32]{2,1,0:T(4,128)S(1)} all-gather(f32[1,3,32]{2,1,0:T(4,128)S(1)} %select_bitcast_fusion), channel_id=1, replica_groups=mesh['tile'=32,'slide'=8] {'tile'}, dimensions={0}, use_global_device_ids=true | all-gather | bytes 12672 | tf_op jit(solution)/shard_map/all_gather | solution.py:71
  63.0 47.3 %all-gather = bf16[32,1,2048]{2,1,0:T(2,128)(2,1)S(1)} all-gather(bf16[1,1,2048]{2,1,0:T(2,128)(2,1)S(1)} %divide_convert_fusion), channel_id=2, replica_groups=mesh['tile'=32,'slide'=8] {'tile'}, dimensions={0}, use_global_device_ids=true | all-gather | bytes 135168 | tf_op jit(solution)/shard_map/all_gather | solution.py:84
  110.6 2.2 reshape.110
  112.9 1.7 fusion.89
  114.6 1.3 reshape_squeeze.39
  116.4 1.3 reshape_squeeze.41
  117.8 1.3 reshape_squeeze.40
  119.1 1.4 reshape_squeeze.38
  120.5 1.3 reshape_squeeze.37
  121.8 1.3 reshape_squeeze.36
  123.1 1.3 reshape_squeeze.44
  124.4 1.4 reshape_squeeze.43
  125.8 2.5 pad_slice_fusion.12
  128.4 3.0 reshape.109
  131.4 2.3 reshape.107
  133.7 2.2 reshape.108
  135.9 1.2 reshape.111
  137.1 2.2 reshape.112
  139.3 3.3 reshape.113
  142.6 3.0 reshape.114
  145.6 3.2 reshape.106
  148.8 4.0 fusion.33
  152.8 1.4 fusion.40
  154.2 1.4 fusion.25
  155.6 1.4 fusion.27
  157.0 1.3 fusion.29
  158.3 1.3 fusion.31
  159.7 1.4 fusion.36
  161.1 2.9 fusion.38
  164.1 6.7 %multiply_convert_fusion = (bf16[3,7,7,32,64]{4,2,1,0,3:T(8,128)(2,1)S(1)}, f32[3,32,64]{2,0,1:T(4,128)S(1)}) fusion(f32[3,32,64]{2,0,1:T(4,128)S(1)} %copy.348, f32[32,3,7,7,64]{4,3,2,1,0:T(8,128)S(1)} %fusion.25, f32[32,3,7,7,64]{4,3,2,1,0:T(8,128)S(1)} %fusion.27, f32[32,3,7,7,64]{4,3,2,1,0:T(8,128)S(1)} %fusion.29, ...), kind=kOutput, calls=%fused_computation.22 | convolution fusion | flops 44249088 | bytes 11149312 | tf_op jit(solution)/shard_map/nhwgi,igo->nhwgo/dot_general | solution.py:21
  170.8 4.2 fusion.21
  175.0 2.4 fusion.19
  177.5 2.4 fusion.17
  179.9 2.4 fusion.15
  182.3 2.4 fusion.13
  184.8 2.4 fusion.11
  187.2 2.6 fusion.9
  189.8 2.5 fusion.7
  192.3 1.4 fusion.23
  194.9 1.5 copy.385
  196.5 1.5 copy.384
  198.0 2.4 copy.383
  200.4 2.3 copy.382
  202.7 2.3 copy.381
  205.0 2.3 copy.380
  207.4 2.3 copy.379
  209.7 2.3 copy.378
  212.1 2.0 constant_dynamic-update-slice_fusion.8
  214.1 1.9 constant_dynamic-update-slice_fusion.7
  221.8 12.9 %copy.450 = f32[9,64,2048]{1,0,2:T(8,128)} copy(f32[9,64,2048]{2,1,0:T(8,128)} %constant_dynamic-update-slice_fusion) | data formatting | bytes 9437184
  234.7 12.6 %reshape.153 = f32[2048,576]{1,0:T(8,128)} reshape(f32[2048,9,64]{2,1,0:T(8,128)} %bitcast.128) | data formatting | bytes 9437184
  247.5 48.3 %all-gather.2 = bf16[32,3,2048]{2,1,0:T(4,128)(2,1)S(1)} all-gather(bf16[1,3,2048]{2,1,0:T(4,128)(2,1)S(1)} %reshape.118), channel_id=1, replica_groups=mesh['tile'=32,'slide'=8] {'tile'}, dimensions={0}, use_global_device_ids=true | all-gather | bytes 405504 | tf_op jit(solution)/shard_map/all_gather | solution.py:75
  297.5 1.2 fusion.2
  298.7 1.3 fusion.3
  300.0 1.3 fusion.4
  301.3 1.2 fusion.5
  303.5 1.2 fusion
  304.8 2.4 fusion.50
  307.2 5.6 %add_bitcast_fusion = f32[3,7,7,32,64]{4,2,1,0,3:T(8,128)} fusion(f32[32,3,7,7,64]{4,3,2,1,0:T(8,128)S(1)} %fusion.6, f32[32,3,7,7,64]{4,3,2,1,0:T(8,128)S(1)} %fusion.5, f32[32,3,7,7,64]{4,3,2,1,0:T(8,128)S(1)} %fusion.4, f32[32,3,7,7,64]{4,3,2,1,0:T(8,128)} %fusion.50, f32[32,3,7,7,64]{4,3,2,1,0:T(8,128)S(1)} %fusion.3, ...), kind=kOutput, calls=%fused_computation.21 | convolution fusion | flops 40943616 | bytes 11702272 | tf_op jit(solution)/shard_map/nhwgo,igo->nhwgi/dot_general | solution.py:50
  312.8 158.3 %reduce-scatter.4.cloned.1.call-done = f32[64,576]{1,0:T(8,128)} async-done(((f32[2048,576]{1,0:T(8,128)}), f32[64,576]{1,0:T(8,128)}) %reduce-scatter.4.cloned.1.call-update) | async-done | bytes 147472
  473.6 2.2 copy.358
  475.8 2.5 broadcast_in_dim_reshape.4
  478.3 60.0 %all-reduce.4.cloned.1.call-done = f32[9,64,64]{2,1,0:T(8,128)} async-done(((f32[9,64,64]{2,1,0:T(8,128)}), f32[9,64,64]{2,1,0:T(8,128)}) %all-reduce.4.cloned.1.call-update) | async-done | bytes 147472 | tf_op jit(solution)/shard_map/psum | solution.py:93
  538.4 1.7 broadcast_multiply_fusion
  (95 shorter events, 16.5 us)
Async XLA Ops:
  7.2 103.5 %copy-start.23 = (bf16[1,3,7,7,2048]{4,3,2,1,0:T(8,128)(2,1)S(1)}, bf16[1,3,7,7,2048]{4,3,2,1,0:T(8,128)(2,1)}, u32[]{:S(2)}) copy-start(bf16[1,3,7,7,2048]{4,3,2,1,0:T(8,128)(2,1)} %param.7) | copy-start | bytes 1806340
  7.2 463.9 %reduce-scatter.4.cloned.1.call-start = ((), (), s32[]{:S(2)}) async-start(), calls=%async_computation.2 | async-start | bytes 5406720
  128.4 3.1 copy-start.24
  139.3 17.7 %copy-start = (bf16[3,7,7,32,64]{4,3,2,1,0:T(8,128)(2,1)}, bf16[3,7,7,32,64]{4,3,2,1,0:T(8,128)(2,1)S(1)}, u32[]{:S(2)}) copy-start(bf16[3,7,7,32,64]{4,3,2,1,0:T(8,128)(2,1)S(1)} %reshape.112) | copy-start | bytes 1806340
  148.8 4.0 copy-start.4
  148.8 4.0 copy-start.15
  152.8 1.4 copy-start.3
  152.8 1.4 copy-start.13
  154.2 1.4 copy-start.2
  154.2 1.4 copy-start.19
  157.0 1.3 copy-start.11
  158.3 1.3 copy-start.7
  158.3 1.4 copy-start.17
  159.7 1.4 copy-start.6
  159.7 1.4 copy-start.21
  170.8 4.3 copy-start.8
  175.0 2.5 copy-start.9
  177.5 2.4 copy-start.31
  182.3 2.4 copy-start.1
  189.8 2.5 copy-start.5
  212.1 3.9 copy-start.30
  212.1 4.8 copy-start.29
  214.1 3.6 copy-start.28
  216.0 2.5 copy-start.27
  216.8 2.5 copy-start.26
  247.4 49.1 %copy-start.22 = (bf16[64,32,64]{2,1,0:T(8,128)(2,1)S(1)}, bf16[64,32,64]{2,1,0:T(8,128)(2,1)}, u32[]{:S(2)}) copy-start(bf16[64,32,64]{2,1,0:T(8,128)(2,1)} %reshape_squeeze.37) | copy-start | bytes 786436
  247.4 291.0 %all-reduce.4.cloned.1.call-start = ((), (), s32[]{:S(2)}) async-start(), calls=%async_computation.1 | async-start | bytes 589824 | tf_op jit(solution)/shard_map/psum | solution.py:93
  296.4 1.1 copy-start.18
  297.5 1.2 copy-start.10
  298.7 1.3 copy-start.12
  301.3 1.2 copy-start.20
  302.5 1.0 copy-start.16
  303.5 1.2 copy-start.25
  304.7 2.4 copy-start.14
Sparse Core Ops, SparseCore 0:
  247.5 223.5 reduce-scatter.3
  474.0 64.3 all-reduce.3
where the time goes:
time: 554 us; the launch traced here: 547 us
  waiting for transfers between devices  218 us (39%)
  blocking collectives  147 us (27%)
  local copies, waits for them, and re-layouts  99.3 us (18%)
  matrix products  61.1 us (11%)
  between operations  16 us (3%)
    unnamed x3, waiting for transfers between devices  158 us
    psum x1, waiting for transfers between devices, shards(): reduced = lax.psum(shard_sum, 'slide')  60 us
    all_gather x1, blocking collectives, shards(): shares = lax.all_gather(routing, 'tile', axis=1, tiled=True)  51.4 us
    all_gather x1, blocking collectives, shards(): lax.all_gather(embedding, 'tile', axis=0, tiled=True).astype(jnp.float32)  48.3 us
    all_gather x1, blocking collectives, shards(): every_scaled = lax.all_gather(scaled, 'tile', axis=0, tiled=True)  47.3 us
    unnamed x79, local copies, waits for them, and re-layouts  37.3 us
    dot_general x9, matrix products, conv_backward(): jnp.einsum('nhwgi,nhwgo->igo', window, grads_split, preferred_element_typ...  22.9 us
    reshape x9, local copies, waits for them, and re-layouts, conv_forward(): padded[:, row_off:row_off + spatial, col_off:col_off + spatial, :]  22.6 us
  transfers between devices with their start and end apart: 2, of which 2 were waited for; matrix products, arithmetic and copies ran while one was open for 4% of the time, Pallas kernels for 0%

commit v1 on v0

--- a/solution.py
+++ b/solution.py
@@ -1,9 +1,19 @@
+import functools
 import jax
 import jax.numpy as jnp
 from jax import lax
 from jax.sharding import PartitionSpec as P
+from jax.lax import all_gather
 
 loss_scale = 512.0
+
+
+def define_threads(load, named_axis):
+    found_now = jnp.sum(all_gather(load, named_axis), axis=0)
+    return found_now
+
+
+field_derive = functools.partial(define_threads, named_axis="slide")
 
 
 def conv_forward(features, weight):
@@ -90,7 +100,7 @@
     pre_grad = (tile_grads[:, None, None, :] / (spatial * spatial) * slope).astype(jnp.bfloat16)
     input_grads, weight_terms = conv_backward(features, conv_weight, pre_grad)
     shard_sum = lax.psum_scatter(weight_terms, "tile", scatter_dimension=2, tiled=True)
-    reduced = lax.psum(shard_sum, "slide")
+    reduced = field_derive(shard_sum)
     return (pooled[None], input_grads[None], reduced / loss_scale)
 
 

time: 554 us -> 518 us (0.935)
  waiting for transfers between devices: 218 us -> 170 us
  local copies, waits for them, and re-layouts: 99.3 us -> 105 us
  matrix products: 61.1 us -> 66.7 us
    psum x1 -> x0, waiting for transfers between devices: 60 us -> none  [shards(): reduced = lax.psum(shard_sum, 'slide')]
    all_gather x0 -> x1, waiting for transfers between devices: none -> 11.1 us  [define_threads(): found_now = jnp.sum(all_gather(load, named_axis), axis=0)]
    dot_general x9, matrix products: 15.9 us -> 24.2 us  [conv_backward(): jnp.einsum('nhwgo,igo->nhwgi', shifted, tap, preferred_element_type=jnp.f...]
    unnamed x79 -> x91, local copies, waits for them, and re-layouts: 37.3 us -> 42.2 us
  transfers between devices with their start and end apart: 2 -> 2, of which waited for: 2 -> 2; matrix products, arithmetic and copies ran while one was open for 4% -> 6% of each run, Pallas kernels for 0% -> 0%
where the time goes in v1:
time: 518 us; the launch traced here: 510 us
  waiting for transfers between devices  170 us (33%)
  blocking collectives  147 us (28%)
  local copies, waits for them, and re-layouts  105 us (20%)
  matrix products  66.7 us (13%)
  between operations  16 us (3%)
  other arithmetic  5.58 us (1%)
    unnamed x3, waiting for transfers between devices  159 us
    all_gather x1, blocking collectives, shards(): shares = lax.all_gather(routing, 'tile', axis=1, tiled=True)  51.4 us
    all_gather x1, blocking collectives, shards(): lax.all_gather(embedding, 'tile', axis=0, tiled=True).astype(jnp.float32)  48.1 us
    all_gather x1, blocking collectives, shards(): every_scaled = lax.all_gather(scaled, 'tile', axis=0, tiled=True)  47.3 us
    unnamed x91, local copies, waits for them, and re-layouts  42.2 us
    dot_general x9, matrix products, conv_backward(): jnp.einsum('nhwgo,igo->nhwgi', shifted, tap, preferred_element_type=jnp.f...  24.2 us
    dot_general x9, matrix products, conv_backward(): jnp.einsum('nhwgi,nhwgo->igo', window, grads_split, preferred_element_typ...  22.7 us
    reshape x9, local copies, waits for them, and re-layouts, conv_forward(): padded[:, row_off:row_off + spatial, col_off:col_off + spatial, :]  22.5 us
  transfers between devices with their start and end apart: 2, of which 2 were waited for; matrix products, arithmetic and copies ran while one was open for 6% of the time, Pallas kernels for 0%

profile of v1, /device:TPU:2, one launch (start us, length us, event | category | flops | bytes accessed | tf_op | source)
XLA Modules:
  0.0 509.7 jit_solution(6165199759344250239)
XLA Ops:
  9.5 51.4 %all-gather.2 = f32[32,3,32]{2,1,0:T(4,128)S(1)} all-gather(f32[1,3,32]{2,1,0:T(4,128)S(1)} %select_bitcast_fusion), channel_id=1, replica_groups=mesh['tile'=32,'slide'=8] {'tile'}, dimensions={0}, use_global_device_ids=true | all-gather | bytes 12672 | tf_op jit(solution)/shard_map/all_gather | solution.py:81
  63.0 47.3 %all-gather = bf16[32,1,2048]{2,1,0:T(2,128)(2,1)S(1)} all-gather(bf16[1,1,2048]{2,1,0:T(2,128)(2,1)S(1)} %divide_convert_fusion), channel_id=2, replica_groups=mesh['tile'=32,'slide'=8] {'tile'}, dimensions={0}, use_global_device_ids=true | all-gather | bytes 135168 | tf_op jit(solution)/shard_map/all_gather | solution.py:94
  110.6 2.2 reshape.110
  112.9 1.8 fusion.89
  114.6 1.3 reshape_squeeze.39
  116.0 1.3 reshape_squeeze.42
  117.3 1.3 reshape_squeeze.41
  118.6 1.3 reshape_squeeze.40
  120.0 1.4 reshape_squeeze.38
  122.7 1.3 reshape_squeeze.36
  124.5 1.4 reshape_squeeze.43
  125.9 2.3 pad_slice_fusion.12
  128.2 3.0 reshape.109
  131.2 2.2 reshape.107
  133.5 2.2 reshape.108
  136.9 2.2 reshape.112
  139.1 3.3 reshape.113
  142.4 3.0 reshape.114
  145.3 3.2 reshape.106
  148.5 4.0 fusion.33
  152.5 1.4 fusion.40
  153.9 1.4 fusion.25
  155.4 1.4 fusion.27
  156.8 1.3 fusion.29
  158.1 1.4 fusion.31
  159.5 1.4 fusion.36
  160.9 1.3 fusion.38
  162.2 5.8 %multiply_convert_fusion = (bf16[3,7,7,32,64]{4,2,1,0,3:T(8,128)(2,1)S(1)}, f32[3,32,64]{2,0,1:T(4,128)S(1)}) fusion(f32[3,32,64]{2,0,1:T(4,128)S(1)} %copy.387, f32[32,3,7,7,64]{4,3,2,1,0:T(8,128)S(1)} %fusion.25, f32[32,3,7,7,64]{4,3,2,1,0:T(8,128)S(1)} %fusion.27, f32[32,3,7,7,64]{4,3,2,1,0:T(8,128)S(1)} %fusion.29, ...), kind=kOutput, calls=%fused_computation.22 | convolution fusion | flops 44249088 | bytes 11149312 | tf_op jit(solution)/shard_map/nhwgi,igo->nhwgo/dot_general | solution.py:31
  168.1 4.3 fusion.21
  172.3 2.4 fusion.19
  174.7 2.5 fusion.17
  177.2 2.4 fusion.15
  179.7 2.5 fusion.13
  182.2 2.4 fusion.11
  184.6 2.4 fusion.9
  187.0 2.4 fusion.7
  189.4 1.4 fusion.23
  192.0 1.5 copy.424
  193.5 1.5 copy.423
  195.1 2.4 copy.422
  197.4 2.3 copy.421
  199.8 2.3 copy.420
  202.1 2.4 copy.419
  204.4 2.3 copy.418
  206.8 2.3 copy.417
  209.1 2.0 constant_dynamic-update-slice_fusion.8
  211.1 2.0 constant_dynamic-update-slice_fusion.7
  218.9 13.0 %copy.491 = f32[9,64,2048]{1,0,2:T(8,128)} copy(f32[9,64,2048]{2,1,0:T(8,128)} %constant_dynamic-update-slice_fusion) | data formatting | bytes 9437184
  232.0 12.6 %reshape.154 = f32[2048,576]{1,0:T(8,128)} reshape(f32[2048,9,64]{2,1,0:T(8,128)} %bitcast.129) | data formatting | bytes 9437184
  244.7 48.1 %all-gather.3 = bf16[32,3,2048]{2,1,0:T(4,128)(2,1)S(1)} all-gather(bf16[1,3,2048]{2,1,0:T(4,128)(2,1)S(1)} %reshape.119), channel_id=1, replica_groups=mesh['tile'=32,'slide'=8] {'tile'}, dimensions={0}, use_global_device_ids=true | all-gather | bytes 405504 | tf_op jit(solution)/shard_map/all_gather | solution.py:85
  293.9 2.4 fusion.1
  296.3 2.8 fusion.2
  299.1 2.9 fusion.3
  301.9 2.8 fusion.4
  304.8 2.8 fusion.5
  307.6 2.4 fusion.6
  310.0 158.5 %reduce-scatter.4.cloned.1.call-done = f32[64,576]{1,0:T(8,128)} async-done(((f32[2048,576]{1,0:T(8,128)}), f32[64,576]{1,0:T(8,128)}) %reduce-scatter.4.cloned.1.call-update) | async-done | bytes 147472
  468.4 1.8 reshape.155
  470.3 1.9 copy.492
  475.9 6.1 %add_bitcast_fusion = f32[3,7,7,32,64]{4,2,1,0,3:T(8,128)S(1)} fusion(f32[32,3,7,7,64]{4,3,2,1,0:T(8,128)} %fusion.6, f32[32,3,7,7,64]{4,3,2,1,0:T(8,128)} %fusion.5, f32[32,3,7,7,64]{4,3,2,1,0:T(8,128)} %fusion.4, f32[32,3,7,7,64]{4,3,2,1,0:T(8,128)S(1)} %fusion.50, f32[32,3,7,7,64]{4,3,2,1,0:T(8,128)S(1)} %copy-done.2, ...), kind=kOutput, calls=%fused_computation.21 | convolution fusion | flops 40943616 | bytes 11702272 | tf_op jit(solution)/shard_map/nhwgo,igo->nhwgi/dot_general | solution.py:60
  482.0 1.9 copy.397
  483.8 3.9 broadcast_in_dim_reshape.4
  488.6 11.1 %all-gather.6.cloned.1.call-done = f32[72,64,64]{2,1,0:T(8,128)} async-done(((f32[9,64,64]{2,1,0:T(8,128)}), f32[72,64,64]{2,1,0:T(8,128)}) %all-gather.6.cloned.1.call-update) | async-done | bytes 1179664 | tf_op jit(solution)/shard_map/all_gather | solution.py:12
  499.7 1.9 reduce_sum.39
  (108 shorter events, 20.3 us)
Async XLA Ops:
  7.2 103.5 %copy-start.28 = (bf16[1,3,7,7,2048]{4,3,2,1,0:T(8,128)(2,1)S(1)}, bf16[1,3,7,7,2048]{4,3,2,1,0:T(8,128)(2,1)}, u32[]{:S(2)}) copy-start(bf16[1,3,7,7,2048]{4,3,2,1,0:T(8,128)(2,1)} %param.7) | copy-start | bytes 1806340
  7.2 461.3 %reduce-scatter.4.cloned.1.call-start = ((), (), s32[]{:S(2)}) async-start(), calls=%async_computation.2 | async-start | bytes 5406720
  139.1 17.7 %copy-start.3 = (bf16[3,7,7,32,64]{4,3,2,1,0:T(8,128)(2,1)}, bf16[3,7,7,32,64]{4,3,2,1,0:T(8,128)(2,1)S(1)}, u32[]{:S(2)}) copy-start(bf16[3,7,7,32,64]{4,3,2,1,0:T(8,128)(2,1)S(1)} %reshape.112) | copy-start | bytes 1806340
  148.5 4.0 copy-start.9
  148.5 4.0 copy-start.15
  152.5 1.4 copy-start.7
  153.9 1.4 copy-start.5
  153.9 1.4 copy-start.24
  155.3 1.4 copy-start.17
  156.8 1.3 copy-start.20
  158.1 1.4 copy-start.12
  158.1 1.4 copy-start.22
  159.5 1.4 copy-start.11
  159.5 1.4 copy-start.26
  168.0 4.3 copy-start.13
  172.3 2.4 copy-start.14
  174.7 2.5 copy-start.36
  179.7 2.5 copy-start.4
  182.2 2.4 copy-start.6
  184.6 2.4 copy-start.8
  187.0 2.4 copy-start.10
  209.1 3.9 copy-start.34
  209.1 4.8 copy-start.33
  211.1 3.6 copy-start.32
  213.1 2.5 copy-start.31
  213.9 2.5 copy-start.30
  244.6 49.3 %copy-start.27 = (bf16[64,32,64]{2,1,0:T(8,128)(2,1)S(1)}, bf16[64,32,64]{2,1,0:T(8,128)(2,1)}, u32[]{:S(2)}) copy-start(bf16[64,32,64]{2,1,0:T(8,128)(2,1)} %reshape_squeeze.37) | copy-start | bytes 786436
  244.6 255.1 %all-gather.6.cloned.1.call-start = ((), (), s32[]{:S(2)}) async-start(), calls=%async_computation.1 | async-start | bytes 2654208 | tf_op jit(solution)/shard_map/all_gather | solution.py:12
  293.9 2.4 copy-start.23
  296.3 2.8 copy-start.19
  299.1 2.9 copy-start.21
  301.9 2.8 copy-start.18
  304.8 2.8 copy-start.25
  307.6 165.8 %copy-start.29 = (bf16[64,32,64]{2,1,0:T(8,128)(2,1)S(1)}, bf16[64,32,64]{2,1,0:T(8,128)(2,1)}, u32[]{:S(2)}) copy-start(bf16[64,32,64]{2,1,0:T(8,128)(2,1)} %reshape_squeeze.40) | copy-start | bytes 786436
  310.0 162.2 %copy-start.16 = (bf16[64,32,64]{2,1,0:T(8,128)(2,1)S(1)}, bf16[64,32,64]{2,1,0:T(8,128)(2,1)}, u32[]{:S(2)}) copy-start(bf16[64,32,64]{2,1,0:T(8,128)(2,1)} %reshape_squeeze.36) | copy-start | bytes 786436
  472.2 2.1 copy-start.1
  472.2 2.6 copy-start.2
  473.4 2.4 copy-start
  483.8 3.9 copy-start.35
Sparse Core Ops, SparseCore 0:
  244.7 223.7 reduce-scatter.3
  472.3 27.3 all-gather.5
